TPU v7x, 512 devices: a whole 4x4x16 slice. The times are simulated.
512 devices in a mesh: gx: 16 (over y_lo, x, core), gy: 32 (over y_hi, z).
Axes of the slice: x: 4, y: 4 (y_hi: 2, y_lo: 2; y = y_hi * 2 + y_lo), z: 16, core: 2. Of those that a mesh axis runs over, the one named last changes fastest.
Arguments:
- phase_field: float32 [16, 2048, 2048], P(None, 'gy', 'gx'), may hold values from -1 to 1
- mobility: float32 [16, 2048, 2048], P(None, 'gy', 'gx'), may hold values from 0.25 to 2.5
- x_inverse: bfloat16 [2048, 2048], P('gx'), may hold values from -2 to 2
- y_inverse: bfloat16 [2048, 2048], P('gy'), may hold values from -2 to 2
Outputs:
- new_phase: float32 [16, 2048, 2048], P(None, 'gy', 'gx')
All inputs are finite; a program needn't handle non-finite values.
Results may differ from a plain program's by a relative error of at most 0.0041.
Values may be sent and summed in bfloat16 or wider, within the bound.
No kernel may reach another device: no remote copies, remote signals or barrier semaphores. Data moves between devices by JAX's collectives and lax.ppermute only.
A program may use at most 64 MiB of HBM per device.

v0:
```python
import jax
import jax.numpy as jnp
from jax import lax
from jax.sharding import Mesh
from jax.sharding import PartitionSpec as P

GY = ("gy_0", "gy_1")


step_size = 0.15


def extended(x, sides, width):
    for axis, dim in sides:
        size, length = (lax.axis_size(axis), x.shape[dim])
        up = [(i, (i + 1) % size) for i in range(size - 1)]
        down = [(j, i) for i, j in up]
        last = lax.slice_in_dim(x, length - width, length, axis=dim)
        leading = lax.slice_in_dim(x, 0, width, axis=dim)
        before = lax.ppermute(last, axis, up)
        after = lax.ppermute(leading, axis, down)
        x = jnp.concatenate([before, x, after], axis=dim)
    return x


def joined_along(parts, dim):
    parts = jnp.moveaxis(parts, 0, dim)
    lengths = parts.shape
    return parts.reshape(*lengths[:dim], lengths[dim] * lengths[dim + 1], *lengths[dim + 2 :])


def gather_in_order(x, axes, turns):
    parts = x
    for k in turns:
        parts = lax.all_gather(parts, axes[k])
    done = turns[::-1]
    back = [done.index(k) for k in range(len(axes))]
    parts = parts.transpose(*back, *range(len(axes), parts.ndim))
    return parts.reshape(-1, *x.shape)


def whole_of(x, axes, turns, dim):
    return joined_along(gather_in_order(x, axes, turns), dim)


def face_mob(center_mob, near_mob):
    return 2.0 * center_mob * near_mob / jnp.maximum(center_mob + near_mob, 0.25)


def laplace(values, mobile):
    values_z = jnp.pad(values, ((1, 1), (0, 0), (0, 0)))
    mobile_z = jnp.pad(mobile, ((1, 1), (0, 0), (0, 0)))
    center = values[:, 1:-1, 1:-1]
    center_mob = mobile[:, 1:-1, 1:-1]
    pairs = [
        (values_z[2:, 1:-1, 1:-1], mobile_z[2:, 1:-1, 1:-1]),
        (values_z[:-2, 1:-1, 1:-1], mobile_z[:-2, 1:-1, 1:-1]),
        (values[:, 2:, 1:-1], mobile[:, 2:, 1:-1]),
        (values[:, :-2, 1:-1], mobile[:, :-2, 1:-1]),
        (values[:, 1:-1, 2:], mobile[:, 1:-1, 2:]),
        (values[:, 1:-1, :-2], mobile[:, 1:-1, :-2]),
    ]
    result = jnp.zeros_like(center)
    for near_val, near_mob in pairs:
        result = result + face_mob(center_mob, near_mob) * (near_val - center)
    return result


def local(phase_field, mobility, x_inverse, y_inverse):
    stacked = jnp.stack((phase_field, mobility))
    padded = extended(stacked, (("gx", 3), (GY, 2)), 2)
    phase_pad = padded[0]
    mob_wide = padded[1]
    mob_near = mob_wide[:, 1:-1, 1:-1]
    first_pad = phase_pad[:, 1:-1, 1:-1] + step_size * laplace(phase_pad, mob_wide)
    first = first_pad[:, 1:-1, 1:-1]
    second = (first + step_size * laplace(first_pad, mob_near)).astype(jnp.bfloat16)
    planes, y_rows, x_rows = second.shape
    rows_inverse = extended(x_inverse, (("gx", 0),), 1)
    out_rows = rows_inverse.shape[0]
    segment = lax.all_gather(second, "gx", axis=2, tiled=True)
    seg_len = segment.shape[2]
    inverse_cols = rows_inverse
    flat = segment.reshape(planes * y_rows, seg_len)
    lines = lax.dot_general(
        flat, inverse_cols, (((1,), (1,)), ((), ())), preferred_element_type=jnp.float32
    )
    solved = lines.reshape(planes, y_rows, out_rows)
    chemical = solved * solved * solved - solved
    chemical_pad = extended(chemical, ((GY, 1),), 1)
    solved_own = solved[:, :, 1:-1]
    updated = (solved_own + step_size * laplace(chemical_pad, mob_near)).astype(jnp.bfloat16)
    segment = whole_of(updated, GY, (0, 1), 1)
    inverse_cols = y_inverse
    return jnp.einsum("yk,zkx->zyx", inverse_cols, segment, preferred_element_type=jnp.float32)


def solution(mesh):
    torus = Mesh(mesh.devices.reshape(mesh.shape["gx"], 2, 16), ("gx", "gy_0", "gy_1"))
    in_specs = (P(None, GY, "gx"), P(None, GY, "gx"), P("gx", None), P(GY, None))
    out_specs = P(None, GY, "gx")
    return jax.shard_map(local, mesh=torus, in_specs=in_specs, out_specs=out_specs, check_vma=False)
```

profile of v0, /device:TPU:1, one launch (start us, length us, event | category | flops | bytes accessed | tf_op | source)
XLA Modules:
  0.0 247.7 jit_solution(7225160158829842463)
XLA Ops:
  6.5 1.9 slice_maximum_fusion
  8.5 0.4 copy.6
  8.8 4.5 %collective-permute-start = (f32[2,16,64,2]{2,1,3,0:T(8,128)S(1)}, f32[2,16,64,2]{2,1,3,0:T(8,128)S(1)}, u32[]{:S(2)}, u32[]{:S(2)}) collective-permute-start(f32[2,16,64,2]{2,1,3,0:T(8,128)S(1)} %copy.6), channel_id=1, source_target_pairs={{0,32},{32,64},{64,96},{96,128},{128,160},{160,192},{192,224},{224... | collective-permute-start | bytes 49160 | tf_op jit(solution)/shard_map/ppermute | solution.py:20
  13.3 0.4 copy.7
  13.7 5.7 %collective-permute-start.1 = (f32[2,16,64,2]{2,1,3,0:T(8,128)S(1)}, f32[2,16,64,2]{2,1,3,0:T(8,128)S(1)}, u32[]{:S(2)}, u32[]{:S(2)}) collective-permute-start(f32[2,16,64,2]{2,1,3,0:T(8,128)S(1)} %copy.7), channel_id=1, source_target_pairs={{32,0},{64,32},{96,64},{128,96},{160,128},{192,160},{224,192},{256... | collective-permute-start | bytes 49160 | tf_op jit(solution)/shard_map/ppermute | solution.py:21
  19.4 0.4 copy.8
  19.8 0.4 collective-permute-done.1
  20.2 0.4 copy.9
  20.7 0.3 pad_maximum_fusion.7
  20.9 2.4 collective-permute-start.2
  23.3 1.3 collective-permute-start.3
  24.6 0.0 collective-permute-done.2
  24.7 4.1 %collective-permute-done.3 = f32[2,16,2,132]{3,2,1,0:T(2,128)S(1)} collective-permute-done((f32[2,16,2,132]{3,2,1,0:T(2,128)S(1)}, f32[2,16,2,132]{3,2,1,0:T(2,128)S(1)}, u32[]{:S(2)}, u32[]{:S(2)}) %collective-permute-start.3) | collective-permute-done | bytes 33824 | tf_op jit(solution)/shard_map/ppermute | solution.py:21
  28.8 1.0 pad_maximum_fusion
  29.8 0.2 slice_bitcast_fusion
  30.0 4.3 %fusion.59 = (f32[16,66,130]{2,1,0:T(8,128)S(1)}, f32[16,66,130]{2,1,0:T(8,128)S(1)}) fusion(f32[16,68,132]{2,1,0:T(8,128)S(1)} %get-tuple-element.7, f32[16,68,132]{2,1,0:T(8,128)S(1)} %get-tuple-element.8), kind=kLoop, calls=%fused_computation.107 | loop fusion | flops 6040320 | bytes 15254016 | tf_op jit(solution)/shard_map/slice | solution.py:54
  34.3 2.6 %fusion.34 = bf16[16,64,128]{2,1,0:T(8,128)(2,1)} fusion(f32[16,66,130]{2,1,0:T(8,128)S(1)} %get-tuple-element.10, f32[16,68,132]{2,1,0:T(8,128)S(1)} %get-tuple-element.7, f32[16,66,130]{2,1,0:T(8,128)S(1)} %get-tuple-element.9), kind=kLoop, calls=%fused_computation.62 | loop fusion | flops 5898240 | bytes 7864320 | tf_op jit(solution)/shard_map/convert_element_type | solution.py:77
  36.9 0.0 all-gather.7.cloned.1.call-start
  37.0 3.1 %collective-permute-start.4 = (bf16[1,2048]{1,0:T(2,128)(2,1)S(1)}, bf16[1,2048]{1,0:T(2,128)(2,1)S(1)}, u32[]{:S(2)}, u32[]{:S(2)}) collective-permute-start(bf16[1,2048]{1,0:T(2,128)(2,1)S(1)} %get-tuple-element.15), channel_id=1, source_target_pairs={{0,32},{32,64},{64,96},{96,128},{128,160},{160,192},{192,224},{224... | collective-permute-start | bytes 12296 | tf_op jit(solution)/shard_map/ppermute | solution.py:20
  40.1 1.9 collective-permute-start.5
  42.0 3.0 %collective-permute-done.5 = bf16[1,2048]{1,0:T(2,128)(2,1)S(1)} collective-permute-done((bf16[1,2048]{1,0:T(2,128)(2,1)S(1)}, bf16[1,2048]{1,0:T(2,128)(2,1)S(1)}, u32[]{:S(2)}, u32[]{:S(2)}) %collective-permute-start.5) | collective-permute-done | bytes 4128 | tf_op jit(solution)/shard_map/ppermute | solution.py:21
  45.1 51.3 %all-gather.5.cloned.1.call-done = bf16[16,64,2048]{2,1,0:T(8,128)(2,1)} async-done(((bf16[16,64,128]{2,1,0:T(8,128)(2,1)}), bf16[16,64,2048]{2,1,0:T(8,128)(2,1)}) %all-gather.5.cloned.1.call-update) | async-done | bytes 4194320 | tf_op jit(solution)/shard_map/all_gather | solution.py:81
  96.3 3.5 %multiply_subtract_fusion = (f32[16,64,130]{2,1,0:T(8,128)S(1)}, f32[16,64,130]{2,1,0:T(8,128)S(1)}) fusion(bf16[16,64,2048]{2,1,0:T(8,128)(2,1)} %all-gather.5.cloned.1.call-done, bf16[1,2048]{1,0:T(2,128)(2,1)S(1)} %collective-permute-done.5, bf16[128,2048]{1,0:T(8,128)(2,1)S(1)} %copy-done.3, bf16[1,2048]{1,0:T(2,128)(2,1)S(1)} %collective-permute-done.4), kind=kOutput, calls=%fused_computation.3 | convolution fusion | flops 547256320 | bytes 5791744 | tf_op jit(solution)/shard_map/dot_general | solution.py:85
  99.8 1.3 collective-permute-start.7
  101.1 4.0 %collective-permute-start.6 = (f32[16,1,130]{2,1,0:T(1,128)S(1)}, f32[16,1,130]{2,1,0:T(1,128)S(1)}, u32[]{:S(2)}, u32[]{:S(2)}) collective-permute-start(f32[16,1,130]{2,1,0:T(1,128)S(1)} %get-tuple-element.12), channel_id=1, source_target_pairs={{0,1},{1,2},{2,3},{3,4},{4,5},{5,6},{6,7},{7,8},{8,9},{9,10},{10,1... | collective-permute-start | bytes 24968 | tf_op jit(solution)/shard_map/ppermute | solution.py:20
  105.1 0.8 collective-permute-done.6
  106.0 0.1 select_maximum_fusion
  106.1 2.1 fusion.41
  108.3 15.0 %all-gather = bf16[32,64,128]{2,1,0:T(8,128)(2,1)} all-gather(bf16[16,64,128]{2,1,0:T(8,128)(2,1)S(1)} %fusion.41), channel_id=2, replica_groups=mesh['gx'=16,'gy_0'=2,'gy_1'=16] {'gy_0'}, dimensions={0}, use_global_device_ids=true | all-gather | bytes 786432 | tf_op jit(solution)/shard_map/all_gather | solution.py:35
  123.2 102.4 %all-gather.7.cloned.1.call-done = bf16[32,16,64,128]{3,2,1,0:T(8,128)(2,1)} async-done(((bf16[2,16,64,128]{3,2,1,0:T(8,128)(2,1)}), bf16[32,16,64,128]{3,2,1,0:T(8,128)(2,1)}) %all-gather.7.cloned.1.call-update) | async-done | bytes 8388624 | tf_op jit(solution)/shard_map/all_gather | solution.py:35
  225.6 9.6 %copy.10 = bf16[2,16,16,64,128]{4,3,1,0,2:T(8,128)(2,1)} copy(bf16[2,16,16,64,128]{4,3,2,0,1:T(8,128)(2,1)} %bitcast.28) | data formatting | bytes 16777216 | tf_op jit(solution)/shard_map/transpose | solution.py:38
  235.2 5.7 %convolution_bitcast_fusion = f32[16,64,128]{2,1,0:T(8,128)} fusion(bf16[16,2048,128]{2,1,0:T(8,128)(2,1)} %bitcast.27, bf16[64,2048]{1,0:T(8,128)(2,1)S(1)} %copy-done), kind=kOutput, calls=%fused_computation.15 | convolution fusion | flops 536870912 | bytes 9175040 | tf_op jit(solution)/shard_map/yk,zkx->zyx/dot_general | solution.py:95
  (16 shorter events, 0.1 us)
Async XLA Ops:
  6.5 228.7 %copy-start = (bf16[64,2048]{1,0:T(8,128)(2,1)S(1)}, bf16[64,2048]{1,0:T(8,128)(2,1)}, u32[]{:S(2)}) copy-start(bf16[64,2048]{1,0:T(8,128)(2,1)} %param.7) | copy-start | bytes 786436
  6.5 89.8 %all-gather.5.cloned.1.call-start = ((), (), s32[]{:S(2)}) async-start(), calls=%async_computation | async-start | bytes 4456448 | tf_op jit(solution)/shard_map/all_gather | solution.py:81
  8.8 10.6 %collective-permute-start = (f32[2,16,64,2]{2,1,3,0:T(8,128)S(1)}, f32[2,16,64,2]{2,1,3,0:T(8,128)S(1)}, u32[]{:S(2)}, u32[]{:S(2)}) collective-permute-start(f32[2,16,64,2]{2,1,3,0:T(8,128)S(1)} %copy.6), channel_id=1, source_target_pairs={{0,32},{32,64},{64,96},{96,128},{128,160},{160,192},{192,224},{224... | collective-permute-start | bytes 49160 | tf_op jit(solution)/shard_map/ppermute | solution.py:20
  13.7 6.9 %copy-start.1 = (f32[16,64,128]{2,1,0:T(8,128)S(1)}, f32[16,64,128]{2,1,0:T(8,128)}, u32[]{:S(2)}) copy-start(f32[16,64,128]{2,1,0:T(8,128)} %param.5) | copy-start | bytes 1572868
  13.7 6.9 %copy-start.2 = (f32[16,64,128]{2,1,0:T(8,128)S(1)}, f32[16,64,128]{2,1,0:T(8,128)}, u32[]{:S(2)}) copy-start(f32[16,64,128]{2,1,0:T(8,128)} %param.4) | copy-start | bytes 1572868
  13.7 6.5 %collective-permute-start.1 = (f32[2,16,64,2]{2,1,3,0:T(8,128)S(1)}, f32[2,16,64,2]{2,1,3,0:T(8,128)S(1)}, u32[]{:S(2)}, u32[]{:S(2)}) collective-permute-start(f32[2,16,64,2]{2,1,3,0:T(8,128)S(1)} %copy.7), channel_id=1, source_target_pairs={{32,0},{64,32},{96,64},{128,96},{160,128},{192,160},{224,192},{256... | collective-permute-start | bytes 49160 | tf_op jit(solution)/shard_map/ppermute | solution.py:21
  20.9 3.7 %collective-permute-start.2 = (f32[2,16,2,132]{3,2,1,0:T(2,128)S(1)}, f32[2,16,2,132]{3,2,1,0:T(2,128)S(1)}, u32[]{:S(2)}, u32[]{:S(2)}) collective-permute-start(f32[2,16,2,132]{3,2,1,0:T(2,128)S(1)} %get-tuple-element.5), channel_id=1, source_target_pairs={{0,1},{1,2},{2,3},{3,4},{4,5},{5,6},{6,7},{7,8},{8,9},{9,10},{10,1... | collective-permute-start | bytes 101384 | tf_op jit(solution)/shard_map/ppermute | solution.py:20
  23.3 5.4 %collective-permute-start.3 = (f32[2,16,2,132]{3,2,1,0:T(2,128)S(1)}, f32[2,16,2,132]{3,2,1,0:T(2,128)S(1)}, u32[]{:S(2)}, u32[]{:S(2)}) collective-permute-start(f32[2,16,2,132]{3,2,1,0:T(2,128)S(1)} %get-tuple-element.6), channel_id=1, source_target_pairs={{1,0},{2,1},{3,2},{4,3},{5,4},{6,5},{7,6},{8,7},{9,8},{10,9},{11,1... | collective-permute-start | bytes 101384 | tf_op jit(solution)/shard_map/ppermute | solution.py:21
  34.3 2.7 %copy-start.3 = (bf16[128,2048]{1,0:T(8,128)(2,1)S(1)}, bf16[128,2048]{1,0:T(8,128)(2,1)}, u32[]{:S(2)}) copy-start(bf16[128,2048]{1,0:T(8,128)(2,1)} %param.6) | copy-start | bytes 1572868
  36.9 188.7 %all-gather.7.cloned.1.call-start = ((), (), s32[]{:S(2)}) async-start(), calls=%async_computation.1 | async-start | bytes 8912896 | tf_op jit(solution)/shard_map/all_gather | solution.py:35
  37.0 5.0 %collective-permute-start.4 = (bf16[1,2048]{1,0:T(2,128)(2,1)S(1)}, bf16[1,2048]{1,0:T(2,128)(2,1)S(1)}, u32[]{:S(2)}, u32[]{:S(2)}) collective-permute-start(bf16[1,2048]{1,0:T(2,128)(2,1)S(1)} %get-tuple-element.15), channel_id=1, source_target_pairs={{0,32},{32,64},{64,96},{96,128},{128,160},{160,192},{192,224},{224... | collective-permute-start | bytes 12296 | tf_op jit(solution)/shard_map/ppermute | solution.py:20
  40.1 5.0 %collective-permute-start.5 = (bf16[1,2048]{1,0:T(2,128)(2,1)S(1)}, bf16[1,2048]{1,0:T(2,128)(2,1)S(1)}, u32[]{:S(2)}, u32[]{:S(2)}) collective-permute-start(bf16[1,2048]{1,0:T(2,128)(2,1)S(1)} %get-tuple-element.16), channel_id=1, source_target_pairs={{32,0},{64,32},{96,64},{128,96},{160,128},{192,160},{224,192},{256... | collective-permute-start | bytes 12296 | tf_op jit(solution)/shard_map/ppermute | solution.py:21
  99.8 5.3 %collective-permute-start.7 = (f32[16,1,130]{2,1,0:T(1,128)S(1)}, f32[16,1,130]{2,1,0:T(1,128)S(1)}, u32[]{:S(2)}, u32[]{:S(2)}) collective-permute-start(f32[16,1,130]{2,1,0:T(1,128)S(1)} %get-tuple-element.11), channel_id=1, source_target_pairs={{1,0},{2,1},{3,2},{4,3},{5,4},{6,5},{7,6},{8,7},{9,8},{10,9},{11,1... | collective-permute-start | bytes 24968 | tf_op jit(solution)/shard_map/ppermute | solution.py:21
  101.1 4.8 %collective-permute-start.6 = (f32[16,1,130]{2,1,0:T(1,128)S(1)}, f32[16,1,130]{2,1,0:T(1,128)S(1)}, u32[]{:S(2)}, u32[]{:S(2)}) collective-permute-start(f32[16,1,130]{2,1,0:T(1,128)S(1)} %get-tuple-element.12), channel_id=1, source_target_pairs={{0,1},{1,2},{2,3},{3,4},{4,5},{5,6},{6,7},{7,8},{8,9},{9,10},{10,1... | collective-permute-start | bytes 24968 | tf_op jit(solution)/shard_map/ppermute | solution.py:20
Sparse Core Ops, SparseCore 0:
  37.0 59.2 all-gather.4
  123.4 102.1 all-gather.6
where the time goes:
time: 248 us
  waiting for transfers between devices  162 us (65%)
  starting transfers between devices  24.2 us (10%)
  blocking collectives  15 us (6%)
  between operations  13.6 us (5%)
  other arithmetic  12.4 us (5%)
  local copies, waits for them, and re-layouts  11.4 us (5%)
  matrix products  9.17 us (4%)
    all_gather x1, waiting for transfers between devices, gather_in_order(): parts = lax.all_gather(parts, axes[k])  102 us
    all_gather x1, waiting for transfers between devices, local(): segment = lax.all_gather(second, 'gx', axis=2, tiled=True)  51.3 us
    all_gather x1, blocking collectives, gather_in_order(): parts = lax.all_gather(parts, axes[k])  15 us
    ppermute x4, starting transfers between devices, extended(): before = lax.ppermute(last, axis, up)  14 us
    ppermute x4, starting transfers between devices, extended(): after = lax.ppermute(leading, axis, down)  10.2 us
    transpose x1, local copies, waits for them, and re-layouts, gather_in_order(): parts = parts.transpose(*back, *range(len(axes), parts.ndim))  9.6 us
    ppermute x4, waiting for transfers between devices, extended(): after = lax.ppermute(leading, axis, down)  7.55 us
    dot_general x1, matrix products, local(): jnp.einsum('yk,zkx->zyx', inverse_cols, segment, preferred_element_type=j...  5.71 us
  transfers between devices with their start and end apart: 10, of which 6 were waited for; matrix products, arithmetic and copies ran while one was open for 0% of the time, Pallas kernels for 0%

commit v1 on v0

v1 whole, which is shorter than its diff:
```python
import jax
import jax.numpy as jnp
from jax import lax
from jax.sharding import Mesh
from jax.sharding import PartitionSpec as P

GX = ("yl", "x", "c")
GY = ("yh", "z")

step_size = 0.15


def extended(x, sides):
    for axis, dim, width in sides:
        size, length = (lax.axis_size(axis), x.shape[dim])
        up = [(i, (i + 1) % size) for i in range(size - 1)]
        down = [(j, i) for i, j in up]
        last = lax.slice_in_dim(x, length - width, length, axis=dim)
        leading = lax.slice_in_dim(x, 0, width, axis=dim)
        before = lax.ppermute(last, axis, up)
        after = lax.ppermute(leading, axis, down)
        x = jnp.concatenate([before, x, after], axis=dim)
    return x


def face_mob(center_mob, near_mob):
    return 2.0 * center_mob * near_mob / jnp.maximum(center_mob + near_mob, 0.25)


def laplace(values, mobile):
    values_z = jnp.pad(values, ((1, 1), (0, 0), (0, 0)))
    mobile_z = jnp.pad(mobile, ((1, 1), (0, 0), (0, 0)))
    center = values[:, 1:-1, 1:-1]
    center_mob = mobile[:, 1:-1, 1:-1]
    pairs = [
        (values_z[2:, 1:-1, 1:-1], mobile_z[2:, 1:-1, 1:-1]),
        (values_z[:-2, 1:-1, 1:-1], mobile_z[:-2, 1:-1, 1:-1]),
        (values[:, 2:, 1:-1], mobile[:, 2:, 1:-1]),
        (values[:, :-2, 1:-1], mobile[:, :-2, 1:-1]),
        (values[:, 1:-1, 2:], mobile[:, 1:-1, 2:]),
        (values[:, 1:-1, :-2], mobile[:, 1:-1, :-2]),
    ]
    result = jnp.zeros_like(center)
    for near_val, near_mob in pairs:
        result = result + face_mob(center_mob, near_mob) * (near_val - center)
    return result


def local(phase_field, mobility, x_inverse, y_inverse):
    planes, cy, cx = phase_field.shape
    order = y_inverse.shape[1]
    half = order // 2
    core, high = lax.axis_index("c"), lax.axis_index("yh")

    part = lax.dynamic_slice_in_dim(y_inverse, core * half, half, axis=1)
    y_mine = lax.all_gather(part, "z", axis=0, tiled=True)
    y_other = lax.ppermute(y_mine, "c", [(0, 1), (1, 0)])

    stacked = jnp.stack((phase_field, mobility))
    padded = extended(stacked, ((GX, 3, 2), (GY, 2, 3)))
    rows = extended(x_inverse, ((GX, 0, 1),))
    x_rows = lax.all_to_all(jnp.broadcast_to(rows[None], (4, *rows.shape)), ("yl", "c"), 0, 0, tiled=True)

    phase_pad, mob = padded[0], padded[1]
    first_pad = phase_pad[:, 1:-1, 1:-1] + step_size * laplace(phase_pad, mob)
    mob_near = mob[:, 1:-1, 1:-1]
    first = first_pad[:, 1:-1, 1:-1]
    second = (first + step_size * laplace(first_pad, mob_near)).astype(jnp.bfloat16)

    quarter = planes // 4
    lines = quarter * (cy + 2)
    send = second.reshape(2, 1, 2, lines, cx)
    send = jnp.broadcast_to(send, (2, 4, 2, lines, cx)).reshape(16, lines, cx)
    got = lax.all_to_all(send, GX, 0, 0, tiled=True)
    wide = x_rows.reshape(4, cx + 2, 16, cx)
    solved = jnp.einsum("slk,bnsk->bln", got, wide, preferred_element_type=jnp.float32)
    edges = solved.reshape(4, quarter, cy + 2, cx + 2)[:, :, 1:-1]
    edges = jnp.stack((edges[..., 0], edges[..., -1]), axis=1).reshape(4, 2 * quarter * cy // cx, cx)
    edge_rows = edges.shape[1]
    back = jnp.concatenate([solved[:, :, 1:-1], jnp.pad(edges, ((0, 0), (0, 8 - edge_rows), (0, 0)))], axis=1)
    back = lax.all_to_all(back, ("yl", "c"), 0, 0, tiled=True)
    solved = back[:, :lines].reshape(planes, cy + 2, cx)
    edges = back[:, lines : lines + edge_rows].reshape(4, 2, quarter, cy)
    edges = edges.transpose(1, 0, 2, 3).reshape(2, planes, cy)
    edges = jnp.pad(edges, ((0, 0), (0, 0), (1, 1)))
    solved_pad = jnp.concatenate([edges[0][..., None], solved, edges[1][..., None]], axis=2)
    chemical = solved_pad * solved_pad * solved_pad - solved_pad
    mob_last = mob[:, 2:-2, 1:-1]
    updated = (solved[:, 1:-1] + step_size * laplace(chemical, mob_last)).astype(jnp.bfloat16)

    mine = lax.all_to_all(updated, "z", 0, 0, tiled=True).reshape(half, cx)
    theirs = lax.ppermute(mine, "yh", [(0, 1), (1, 0)])
    same = core == high
    near = jnp.where(same, mine, theirs)
    far = jnp.where(same, theirs, mine)
    dot = lambda a, b: jnp.dot(a, b, preferred_element_type=jnp.float32)
    out = (dot(y_mine, near) + dot(y_other, far)).astype(jnp.bfloat16)
    out = lax.all_to_all(out.reshape(16, cy, cx), "z", 0, 0, tiled=True)
    return out.astype(jnp.float32)


def solution(mesh):
    shape = (2, mesh.shape["gx"] // 4, 2, 2, mesh.shape["gy"] // 2)
    torus = Mesh(mesh.devices.reshape(shape), ("yl", "x", "c", "yh", "z"))
    in_specs = (P(None, GY, GX), P(None, GY, GX), P(GX, None), P(GY, None))
    return jax.shard_map(local, mesh=torus, in_specs=in_specs, out_specs=P(None, GY, GX), check_vma=False)
```

time: 248 us -> 201 us (0.81)
  the two profiles are of different devices: /device:TPU:1 before, /device:TPU:16 now
where the time goes in v1:
time: 201 us; the launch traced here: 200 us
  blocking collectives  52.6 us (26%)
  waiting for transfers between devices  47.1 us (23%)
  starting transfers between devices  44.4 us (22%)
  local copies, waits for them, and re-layouts  19.9 us (10%)
  other arithmetic  16.1 us (8%)
  between operations  13.7 us (7%)
  matrix products  6.24 us (3%)
    all_to_all x1, blocking collectives, local(): mine = lax.all_to_all(updated, 'z', 0, 0, tiled=True).reshape(half, cx)  26.9 us
    all_to_all x1, blocking collectives, local(): out = lax.all_to_all(out.reshape(16, cy, cx), 'z', 0, 0, tiled=True)  25.7 us
    all_to_all x1, waiting for transfers between devices, local(): lax.all_to_all(jnp.broadcast_to(rows[None], (4, *rows.shape)), ('yl', 'c'...  18.6 us
    all_to_all x1, waiting for transfers between devices, local(): got = lax.all_to_all(send, GX, 0, 0, tiled=True)  12.5 us
    ppermute x3, starting transfers between devices, extended(): after = lax.ppermute(leading, axis, down)  11.9 us
    all_to_all x1, starting transfers between devices, local(): lax.all_to_all(jnp.broadcast_to(rows[None], (4, *rows.shape)), ('yl', 'c'...  10.2 us
    ppermute x3, starting transfers between devices, extended(): before = lax.ppermute(last, axis, up)  9.85 us
    all_to_all x1, waiting for transfers between devices, local(): back = lax.all_to_all(back, ('yl', 'c'), 0, 0, tiled=True)  8.75 us
  transfers between devices with their start and end apart: 12, of which 4 were waited for; matrix products, arithmetic and copies ran while one was open for 18% of the time, Pallas kernels for 0%

profile of v1, /device:TPU:16, one launch (start us, length us, event | category | flops | bytes accessed | tf_op | source)
XLA Modules:
  0.0 200.0 jit_solution(15162806153217479102)
XLA Ops:
  6.5 2.0 slice_maximum_fusion
  8.9 1.7 collective-permute-start.2
  11.0 1.3 collective-permute-start.3
  12.3 1.4 fusion.74
  13.7 4.3 %collective-permute-start = (bf16[1,2048]{1,0:T(2,128)(2,1)}, bf16[1,2048]{1,0:T(2,128)(2,1)S(1)}, u32[]{:S(2)}, u32[]{:S(2)}) collective-permute-start(bf16[1,2048]{1,0:T(2,128)(2,1)} %get-tuple-element.15), channel_id=1, source_target_pairs={{0,32},{32,64},{64,96},{96,128},{128,160},{160,192},{192,224},{224... | collective-permute-start | bytes 12296 | tf_op jit(solution)/shard_map/ppermute | solution.py:20
  18.0 1.3 collective-permute-start.1
  22.2 3.8 %collective-permute-start.4 = (f32[2,16,3,132]{3,2,1,0:T(4,128)}, f32[2,16,3,132]{3,2,1,0:T(4,128)S(1)}, u32[]{:S(2)}, u32[]{:S(2)}) collective-permute-start(f32[2,16,3,132]{3,2,1,0:T(4,128)} %get-tuple-element.5), channel_id=1, source_target_pairs={{0,1},{1,2},{2,3},{3,4},{4,5},{5,6},{6,7},{7,8},{8,9},{9,10},{10,1... | collective-permute-start | bytes 152072 | tf_op jit(solution)/shard_map/ppermute | solution.py:20
  26.0 9.3 %collective-permute-start.5 = (f32[2,16,3,132]{3,2,1,0:T(4,128)}, f32[2,16,3,132]{3,2,1,0:T(4,128)}, u32[]{:S(2)}, u32[]{:S(2)}) collective-permute-start(f32[2,16,3,132]{3,2,1,0:T(4,128)} %get-tuple-element.6), channel_id=1, source_target_pairs={{1,0},{2,1},{3,2},{4,3},{5,4},{6,5},{7,6},{8,7},{9,8},{10,9},{11,1... | collective-permute-start | bytes 152072 | tf_op jit(solution)/shard_map/ppermute | solution.py:21
  35.5 1.7 broadcast_in_dim.6
  37.1 10.2 %all-to-all-start = ((bf16[4,130,2048]{2,1,0:T(8,128)(2,1)}), bf16[4,130,2048]{2,1,0:T(8,128)(2,1)}, u32[]{:S(2)}, u32[]{:S(2)}) async-start(bf16[4,130,2048]{2,1,0:T(8,128)(2,1)} %broadcast_in_dim.6), calls=%async_computation | async-start | bytes 4456448 | tf_op jit(solution)/shard_map/all_to_all | solution.py:62
  47.3 1.9 pad_maximum_fusion
  49.4 4.3 %fusion.73 = (f32[16,68,130]{2,1,0:T(8,128)S(1)}, f32[16,68,130]{2,1,0:T(8,128)S(1)}) fusion(f32[16,70,132]{2,1,0:T(8,128)S(1)} %get-tuple-element.7, f32[16,70,132]{2,1,0:T(8,128)S(1)} %get-tuple-element.8), kind=kLoop, calls=%fused_computation.127 | loop fusion | flops 6223360 | bytes 15287296 | tf_op jit(solution)/shard_map/slice | solution.py:34
  53.7 2.1 %fusion.35 = bf16[16,66,128]{2,1,0:T(8,128)(2,1)S(1)} fusion(f32[16,68,130]{2,1,0:T(8,128)S(1)} %get-tuple-element.10, f32[16,70,132]{2,1,0:T(8,128)S(1)} %get-tuple-element.7, f32[16,68,130]{2,1,0:T(8,128)S(1)} %get-tuple-element.9), kind=kLoop, calls=%fused_computation.62 | loop fusion | flops 6082560 | bytes 8527872 | tf_op jit(solution)/shard_map/convert_element_type | solution.py:68
  55.9 18.6 %all-to-all-done = bf16[4,130,2048]{2,1,0:T(8,128)(2,1)} async-done(((bf16[4,130,2048]{2,1,0:T(8,128)(2,1)}), bf16[4,130,2048]{2,1,0:T(8,128)(2,1)}, u32[]{:S(2)}, u32[]{:S(2)}) %all-to-all-start) | async-done | bytes 2129952 | tf_op jit(solution)/shard_map/all_to_all | solution.py:62
  74.5 1.2 broadcast_in_dim.15
  75.7 4.4 %all-to-all-start.1 = ((bf16[16,264,128]{2,1,0:T(8,128)(2,1)}), bf16[16,264,128]{2,1,0:T(8,128)(2,1)}, u32[]{:S(2)}, u32[]{:S(2)}) async-start(bf16[16,264,128]{2,1,0:T(8,128)(2,1)} %bitcast.4), calls=%async_computation.1 | async-start | bytes 2162688 | tf_op jit(solution)/shard_map/all_to_all | solution.py:74
  80.1 4.3 %reshape.30 = bf16[4,130,16,128]{3,2,1,0:T(8,128)(2,1)} reshape(bf16[4,130,2048]{2,1,0:T(8,128)(2,1)} %all-to-all-done) | data formatting | bytes 4259840 | tf_op jit(solution)/shard_map/reshape | solution.py:75
  84.4 12.5 %all-to-all-done.1 = bf16[16,264,128]{2,1,0:T(8,128)(2,1)} async-done(((bf16[16,264,128]{2,1,0:T(8,128)(2,1)}), bf16[16,264,128]{2,1,0:T(8,128)(2,1)}, u32[]{:S(2)}, u32[]{:S(2)}) %all-to-all-start.1) | async-done | bytes 1081376 | tf_op jit(solution)/shard_map/all_to_all | solution.py:74
  96.9 3.2 %fusion.2 = f32[4,264,130]{1,2,0:T(8,128)S(1)} fusion(bf16[4,130,16,128]{3,2,1,0:T(8,128)(2,1)} %reshape.30, bf16[16,264,128]{2,1,0:T(8,128)(2,1)} %all-to-all-done.1), kind=kOutput, calls=%fused_computation.16 | convolution fusion | flops 562298880 | bytes 3760384 | tf_op jit(solution)/shard_map/slk,bnsk->bln/dot_general | solution.py:76
  100.1 1.6 reshape.32
  104.1 3.5 %all-to-all-start.2 = ((f32[4,272,128]{2,1,0:T(8,128)}), f32[4,272,128]{2,1,0:T(8,128)S(1)}, u32[]{:S(2)}, u32[]{:S(2)}) async-start(f32[4,272,128]{2,1,0:T(8,128)} %copy.40), calls=%async_computation.2 | async-start | bytes 1114112 | tf_op jit(solution)/shard_map/all_to_all | solution.py:81
  108.0 8.8 %all-to-all-done.2 = f32[4,272,128]{2,1,0:T(8,128)S(1)} async-done(((f32[4,272,128]{2,1,0:T(8,128)}), f32[4,272,128]{2,1,0:T(8,128)S(1)}, u32[]{:S(2)}, u32[]{:S(2)}) %all-to-all-start.2) | async-done | bytes 557088 | tf_op jit(solution)/shard_map/all_to_all | solution.py:81
  116.9 2.1 %collective-permute-start.7 = (bf16[1024,1024]{1,0:T(8,128)(2,1)}, bf16[1024,1024]{1,0:T(8,128)(2,1)}, u32[]{:S(2)}, u32[]{:S(2)}) collective-permute-start(bf16[1024,1024]{1,0:T(8,128)(2,1)} %all-gather.2.cloned.1.call-done), channel_id=1, source_target_pairs={{0,32},{32,0},{1,33},{33,1},{2,34},{34,2},{3,35},{35,3},{4,36},{36... | collective-permute-start | bytes 6291464 | tf_op jit(solution)/shard_map/ppermute | solution.py:57
  121.0 1.1 copy.42
  122.1 1.1 copy.43
  123.2 1.8 multiply_subtract_fusion
  125.0 1.9 fusion.55
  126.9 26.9 %all_to_all.25 = bf16[16,64,128]{2,1,0:T(8,128)(2,1)S(1)} all-to-all(bf16[16,64,128]{2,1,0:T(8,128)(2,1)S(1)} %fusion.55), channel_id=1, replica_groups=mesh['yl'=2,'x'=4,'c'=2,'yh'=2,'z'=16] {'z'}, dimensions={0} | all-to-all | bytes 524288 | tf_op jit(solution)/shard_map/all_to_all | solution.py:91
  153.8 2.5 %collective-permute-start.6 = (bf16[1024,128]{1,0:T(8,128)(2,1)S(1)}, bf16[1024,128]{1,0:T(8,128)(2,1)S(1)}, u32[]{:S(2)}, u32[]{:S(2)}) collective-permute-start(bf16[1024,128]{1,0:T(8,128)(2,1)S(1)} %bitcast.39), channel_id=1, source_target_pairs={{0,16},{16,0},{1,17},{17,1},{2,18},{18,2},{3,19},{19,3},{4,20},{20... | collective-permute-start | bytes 786440 | tf_op jit(solution)/shard_map/ppermute | solution.py:92
  156.4 7.2 %collective-permute-done.6 = bf16[1024,128]{1,0:T(8,128)(2,1)S(1)} collective-permute-done((bf16[1024,128]{1,0:T(8,128)(2,1)S(1)}, bf16[1024,128]{1,0:T(8,128)(2,1)S(1)}, u32[]{:S(2)}, u32[]{:S(2)}) %collective-permute-start.6) | collective-permute-done | bytes 262176 | tf_op jit(solution)/shard_map/ppermute | solution.py:92
  163.6 2.3 %fusion.66 = f32[1024,128]{1,0:T(8,128)S(1)} fusion(bf16[1024,1024]{1,0:T(8,128)(2,1)} %collective-permute-done.7, bf16[1024,128]{1,0:T(8,128)(2,1)S(1)} %collective-permute-done.6, bf16[1024,128]{1,0:T(8,128)(2,1)S(1)} %bitcast.40, pred[]{:T(512)S(6)} %eq.3), kind=kOutput, calls=%fused_computation.110 | convolution fusion | flops 268566528 | bytes 3145729 | tf_op jit(solution)/shard_map/dot_general | solution.py:96
  166.6 25.7 %all_to_all.26 = bf16[16,64,128]{2,1,0:T(8,128)(2,1)S(1)} all-to-all(bf16[16,64,128]{2,1,0:T(8,128)(2,1)S(1)} %bitcast.42), channel_id=1, replica_groups=mesh['yl'=2,'x'=4,'c'=2,'yh'=2,'z'=16] {'z'}, dimensions={0} | all-to-all | bytes 524288 | tf_op jit(solution)/shard_map/all_to_all | solution.py:98
  (46 shorter events, 10.4 us)
Async XLA Ops:
  6.5 12.8 %copy-start = (bf16[64,2048]{1,0:T(8,128)(2,1)S(1)}, bf16[64,2048]{1,0:T(8,128)(2,1)}, u32[]{:S(2)}) copy-start(bf16[64,2048]{1,0:T(8,128)(2,1)} %param.7) | copy-start | bytes 786436
  6.5 110.3 %all-gather.2.cloned.1.call-start = ((), (), s32[]{:S(2)}) async-start(), calls=%async_computation.5 | async-start | bytes 2228224 | tf_op jit(solution)/shard_map/all_gather | solution.py:56
  8.9 11.1 %collective-permute-start.2 = (f32[2,16,64,2]{2,1,3,0:T(8,128)S(1)}, f32[2,16,64,2]{2,1,3,0:T(8,128)S(1)}, u32[]{:S(2)}, u32[]{:S(2)}) collective-permute-start(f32[2,16,64,2]{2,1,3,0:T(8,128)S(1)} %copy.32), channel_id=1, source_target_pairs={{0,32},{32,64},{64,96},{96,128},{128,160},{160,192},{192,224},{224... | collective-permute-start | bytes 49160 | tf_op jit(solution)/shard_map/ppermute | solution.py:20
  11.0 9.4 %collective-permute-start.3 = (f32[2,16,64,2]{2,1,3,0:T(8,128)S(1)}, f32[2,16,64,2]{2,1,3,0:T(8,128)S(1)}, u32[]{:S(2)}, u32[]{:S(2)}) collective-permute-start(f32[2,16,64,2]{2,1,3,0:T(8,128)S(1)} %copy.33), channel_id=1, source_target_pairs={{32,0},{64,32},{96,64},{128,96},{160,128},{192,160},{224,192},{256... | collective-permute-start | bytes 49160 | tf_op jit(solution)/shard_map/ppermute | solution.py:21
  13.7 21.6 %collective-permute-start = (bf16[1,2048]{1,0:T(2,128)(2,1)}, bf16[1,2048]{1,0:T(2,128)(2,1)S(1)}, u32[]{:S(2)}, u32[]{:S(2)}) collective-permute-start(bf16[1,2048]{1,0:T(2,128)(2,1)} %get-tuple-element.15), channel_id=1, source_target_pairs={{0,32},{32,64},{64,96},{96,128},{128,160},{160,192},{192,224},{224... | collective-permute-start | bytes 12296 | tf_op jit(solution)/shard_map/ppermute | solution.py:20
  18.0 17.3 %collective-permute-start.1 = (bf16[1,2048]{1,0:T(2,128)(2,1)}, bf16[1,2048]{1,0:T(2,128)(2,1)S(1)}, u32[]{:S(2)}, u32[]{:S(2)}) collective-permute-start(bf16[1,2048]{1,0:T(2,128)(2,1)} %get-tuple-element.16), channel_id=1, source_target_pairs={{32,0},{64,32},{96,64},{128,96},{160,128},{192,160},{224,192},{256... | collective-permute-start | bytes 12296 | tf_op jit(solution)/shard_map/ppermute | solution.py:21
  20.0 1.0 copy-start.1
  20.0 1.2 copy-start.2
  21.2 14.1 %copy-start.4 = (bf16[128,2048]{1,0:T(8,128)(2,1)S(1)}, bf16[128,2048]{1,0:T(8,128)(2,1)}, u32[]{:S(2)}) copy-start(bf16[128,2048]{1,0:T(8,128)(2,1)} %param.6) | copy-start | bytes 1572868
  22.2 25.1 %collective-permute-start.4 = (f32[2,16,3,132]{3,2,1,0:T(4,128)}, f32[2,16,3,132]{3,2,1,0:T(4,128)S(1)}, u32[]{:S(2)}, u32[]{:S(2)}) collective-permute-start(f32[2,16,3,132]{3,2,1,0:T(4,128)} %get-tuple-element.5), channel_id=1, source_target_pairs={{0,1},{1,2},{2,3},{3,4},{4,5},{5,6},{6,7},{7,8},{8,9},{9,10},{10,1... | collective-permute-start | bytes 152072 | tf_op jit(solution)/shard_map/ppermute | solution.py:20
  26.0 21.3 %collective-permute-start.5 = (f32[2,16,3,132]{3,2,1,0:T(4,128)}, f32[2,16,3,132]{3,2,1,0:T(4,128)}, u32[]{:S(2)}, u32[]{:S(2)}) collective-permute-start(f32[2,16,3,132]{3,2,1,0:T(4,128)} %get-tuple-element.6), channel_id=1, source_target_pairs={{1,0},{2,1},{3,2},{4,3},{5,4},{6,5},{7,6},{8,7},{9,8},{10,9},{11,1... | collective-permute-start | bytes 152072 | tf_op jit(solution)/shard_map/ppermute | solution.py:21
  37.1 37.3 %all-to-all-start = ((bf16[4,130,2048]{2,1,0:T(8,128)(2,1)}), bf16[4,130,2048]{2,1,0:T(8,128)(2,1)}, u32[]{:S(2)}, u32[]{:S(2)}) async-start(bf16[4,130,2048]{2,1,0:T(8,128)(2,1)} %broadcast_in_dim.6), calls=%async_computation | async-start | bytes 4456448 | tf_op jit(solution)/shard_map/all_to_all | solution.py:62
  75.7 21.2 %all-to-all-start.1 = ((bf16[16,264,128]{2,1,0:T(8,128)(2,1)}), bf16[16,264,128]{2,1,0:T(8,128)(2,1)}, u32[]{:S(2)}, u32[]{:S(2)}) async-start(bf16[16,264,128]{2,1,0:T(8,128)(2,1)} %bitcast.4), calls=%async_computation.1 | async-start | bytes 2162688 | tf_op jit(solution)/shard_map/all_to_all | solution.py:74
  104.1 12.6 %all-to-all-start.2 = ((f32[4,272,128]{2,1,0:T(8,128)}), f32[4,272,128]{2,1,0:T(8,128)S(1)}, u32[]{:S(2)}, u32[]{:S(2)}) async-start(f32[4,272,128]{2,1,0:T(8,128)} %copy.40), calls=%async_computation.2 | async-start | bytes 1114112 | tf_op jit(solution)/shard_map/all_to_all | solution.py:81
  116.9 46.7 %collective-permute-start.7 = (bf16[1024,1024]{1,0:T(8,128)(2,1)}, bf16[1024,1024]{1,0:T(8,128)(2,1)}, u32[]{:S(2)}, u32[]{:S(2)}) collective-permute-start(bf16[1024,1024]{1,0:T(8,128)(2,1)} %all-gather.2.cloned.1.call-done), channel_id=1, source_target_pairs={{0,32},{32,0},{1,33},{33,1},{2,34},{34,2},{3,35},{35,3},{4,36},{36... | collective-permute-start | bytes 6291464 | tf_op jit(solution)/shard_map/ppermute | solution.py:57
  153.8 9.8 %collective-permute-start.6 = (bf16[1024,128]{1,0:T(8,128)(2,1)S(1)}, bf16[1024,128]{1,0:T(8,128)(2,1)S(1)}, u32[]{:S(2)}, u32[]{:S(2)}) collective-permute-start(bf16[1024,128]{1,0:T(8,128)(2,1)S(1)} %bitcast.39), channel_id=1, source_target_pairs={{0,16},{16,0},{1,17},{17,1},{2,18},{18,2},{3,19},{19,3},{4,20},{20... | collective-permute-start | bytes 786440 | tf_op jit(solution)/shard_map/ppermute | solution.py:92
  156.4 9.5 %copy-start.3 = (bf16[1024,1024]{1,0:T(8,128)(2,1)S(1)}, bf16[1024,1024]{1,0:T(8,128)(2,1)}, u32[]{:S(2)}) copy-start(bf16[1024,1024]{1,0:T(8,128)(2,1)} %all-gather.2.cloned.1.call-done) | copy-start | bytes 6291460
Sparse Core Ops, SparseCore 0:
  20.1 81.0 all-gather.1

commit v2 on v1

--- a/solution.py
+++ b/solution.py
@@ -1,6 +1,8 @@
 import jax
 import jax.numpy as jnp
 from jax import lax
+from jax.experimental import pallas as pl
+from jax.experimental.pallas import tpu as pltpu
 from jax.sharding import Mesh
 from jax.sharding import PartitionSpec as P
 
@@ -46,6 +48,36 @@
     return result
 
 
+NT = (((1,), (1,)), ((), ()))
+VMEM = pl.BlockSpec(memory_space=pltpu.VMEM)
+
+
+def solve_x_kernel(block_ref, got_ref, x0_ref, x1_ref, x2_ref, x3_ref, out_ref):
+    own = block_ref[0]
+    parts, lines, cx = got_ref.shape
+    main = lines - 16
+    a = jnp.concatenate([got_ref[s] for s in range(parts)], axis=1)
+    for turn, x_ref in enumerate((x0_ref, x1_ref, x2_ref, x3_ref)):
+        block = own ^ turn
+        m = lax.dot_general(a, x_ref[:cx], NT, preferred_element_type=jnp.float32)
+        out_ref[block, : main + 8] = m[: main + 8]
+        e = lax.dot_general(x_ref[cx:], a[:main], NT, preferred_element_type=jnp.float32)
+        out_ref[block, main + 8 : main + 10] = e[:2, :cx]
+        out_ref[block, main + 10 : main + 12] = e[:2, cx:]
+        out_ref[block, main + 12 :] = jnp.zeros((4, cx), jnp.float32)
+
+
+def solve_x(block, got, x_blocks):
+    parts, lines, cx = got.shape
+    return pl.pallas_call(
+        solve_x_kernel,
+        out_shape=jax.ShapeDtypeStruct((4, lines, cx), jnp.float32),
+        in_specs=[pl.BlockSpec(memory_space=pltpu.SMEM)] + [VMEM] * 5,
+        out_specs=VMEM,
+        name="solve_x",
+    )(block, got, *x_blocks)
+
+
 def local(phase_field, mobility, x_inverse, y_inverse):
     planes, cy, cx = phase_field.shape
     order = y_inverse.shape[1]
@@ -59,7 +91,10 @@
     stacked = jnp.stack((phase_field, mobility))
     padded = extended(stacked, ((GX, 3, 2), (GY, 2, 3)))
     rows = extended(x_inverse, ((GX, 0, 1),))
-    x_rows = lax.all_to_all(jnp.broadcast_to(rows[None], (4, *rows.shape)), ("yl", "c"), 0, 0, tiled=True)
+    rows = jnp.concatenate([rows[1:-1], rows[:1], rows[-1:], jnp.zeros((14, order), rows.dtype)], axis=0)
+    swap = [(0, 1), (1, 0)]
+    rows_yl = lax.ppermute(rows, "yl", swap)
+    x_blocks = (rows, lax.ppermute(rows, "c", swap), rows_yl, lax.ppermute(rows_yl, "c", swap))
 
     phase_pad, mob = padded[0], padded[1]
     first_pad = phase_pad[:, 1:-1, 1:-1] + step_size * laplace(phase_pad, mob)
@@ -68,19 +103,21 @@
     second = (first + step_size * laplace(first_pad, mob_near)).astype(jnp.bfloat16)
 
     quarter = planes // 4
-    lines = quarter * (cy + 2)
-    send = second.reshape(2, 1, 2, lines, cx)
+    main = quarter * cy
+    body = second[:, 1:-1].reshape(4, main, cx)
+    rims = jnp.stack((second[:, 0], second[:, -1]), axis=1).reshape(4, 2 * quarter, cx)
+    send = jnp.concatenate([body, rims, jnp.zeros((4, 16 - 2 * quarter, cx), body.dtype)], axis=1)
+    lines = send.shape[1]
+    send = send.reshape(2, 1, 2, lines, cx)
     send = jnp.broadcast_to(send, (2, 4, 2, lines, cx)).reshape(16, lines, cx)
     got = lax.all_to_all(send, GX, 0, 0, tiled=True)
-    wide = x_rows.reshape(4, cx + 2, 16, cx)
-    solved = jnp.einsum("slk,bnsk->bln", got, wide, preferred_element_type=jnp.float32)
-    edges = solved.reshape(4, quarter, cy + 2, cx + 2)[:, :, 1:-1]
-    edges = jnp.stack((edges[..., 0], edges[..., -1]), axis=1).reshape(4, 2 * quarter * cy // cx, cx)
-    edge_rows = edges.shape[1]
-    back = jnp.concatenate([solved[:, :, 1:-1], jnp.pad(edges, ((0, 0), (0, 8 - edge_rows), (0, 0)))], axis=1)
+    block = (lax.axis_index("yl") * 2 + core).reshape(1).astype(jnp.int32)
+    back = solve_x(block, got, x_blocks)
     back = lax.all_to_all(back, ("yl", "c"), 0, 0, tiled=True)
-    solved = back[:, :lines].reshape(planes, cy + 2, cx)
-    edges = back[:, lines : lines + edge_rows].reshape(4, 2, quarter, cy)
+    body = back[:, :main].reshape(planes, cy, cx)
+    rims = back[:, main : main + 2 * quarter].reshape(planes, 2, cx)
+    solved = jnp.concatenate([rims[:, :1], body, rims[:, 1:]], axis=1)
+    edges = back[:, main + 8 : main + 12].reshape(4, 2, 2, 2, cy).transpose(0, 2, 1, 3, 4).reshape(4, 2, quarter, cy)
     edges = edges.transpose(1, 0, 2, 3).reshape(2, planes, cy)
     edges = jnp.pad(edges, ((0, 0), (0, 0), (1, 1)))
     solved_pad = jnp.concatenate([edges[0][..., None], solved, edges[1][..., None]], axis=2)

time: 201 us -> 182 us (0.905)
  the two profiles are of different devices: /device:TPU:16 before, /device:TPU:2 now
where the time goes in v2:
time: 182 us; the launch traced here: 181 us
  blocking collectives  52.1 us (29%)
  waiting for transfers between devices  41.9 us (23%)
  starting transfers between devices  41.8 us (23%)
  other arithmetic  14.1 us (8%)
  between operations  13.8 us (8%)
  local copies, waits for them, and re-layouts  9.03 us (5%)
  Pallas kernels  5.1 us (3%)
  matrix products  3.03 us (2%)
    all_to_all x1, blocking collectives, local(): mine = lax.all_to_all(updated, 'z', 0, 0, tiled=True).reshape(half, cx)  26.4 us
    all_to_all x1, blocking collectives, local(): out = lax.all_to_all(out.reshape(16, cy, cx), 'z', 0, 0, tiled=True)  25.7 us
    all_gather x1, waiting for transfers between devices, local(): y_mine = lax.all_gather(part, 'z', axis=0, tiled=True)  17 us
    ppermute x3, starting transfers between devices, extended(): after = lax.ppermute(leading, axis, down)  10.5 us
    all_to_all x1, waiting for transfers between devices, local(): got = lax.all_to_all(send, GX, 0, 0, tiled=True)  9.86 us
    all_to_all x1, waiting for transfers between devices, local(): back = lax.all_to_all(back, ('yl', 'c'), 0, 0, tiled=True)  8.75 us
    all_to_all x1, starting transfers between devices, local(): got = lax.all_to_all(send, GX, 0, 0, tiled=True)  7.41 us
    ppermute x3, starting transfers between devices, extended(): before = lax.ppermute(last, axis, up)  5.78 us
  transfers between devices with their start and end apart: 14, of which 5 were waited for; matrix products, arithmetic and copies ran while one was open for 10% of the time, Pallas kernels for 3%

profile of v2, /device:TPU:2, one launch (start us, length us, event | category | flops | bytes accessed | tf_op | source)
XLA Modules:
  0.0 180.7 jit_solution(15601543879323275524)
XLA Ops:
  6.5 1.9 %slice_maximum_fusion = (f32[2,16,64,2]{3,2,1,0:T(8,128)S(1)}, f32[2,16,64,2]{3,2,1,0:T(8,128)S(1)}) fusion(f32[1,16,64,128]{3,2,1,0:T(8,128)} %bitcast.30, f32[1,16,64,128]{3,2,1,0:T(8,128)} %bitcast.33), kind=kLoop, calls=%fused_computation.46 | loop fusion | flops 8192 | bytes 1081344 | tf_op jit(solution)/shard_map/stack | solution.py:91
  8.8 1.9 %collective-permute-start = (f32[2,16,64,2]{2,1,3,0:T(8,128)S(1)}, f32[2,16,64,2]{2,1,3,0:T(8,128)S(1)}, u32[]{:S(2)}, u32[]{:S(2)}) collective-permute-start(f32[2,16,64,2]{2,1,3,0:T(8,128)S(1)} %copy.29), channel_id=1, source_target_pairs={{0,32},{32,64},{64,96},{96,128},{128,160},{160,192},{192,224},{224... | collective-permute-start | bytes 49160 | tf_op jit(solution)/shard_map/ppermute | solution.py:22
  11.1 3.6 %collective-permute-start.1 = (f32[2,16,64,2]{2,1,3,0:T(8,128)S(1)}, f32[2,16,64,2]{2,1,3,0:T(8,128)S(1)}, u32[]{:S(2)}, u32[]{:S(2)}) collective-permute-start(f32[2,16,64,2]{2,1,3,0:T(8,128)S(1)} %copy.30), channel_id=1, source_target_pairs={{32,0},{64,32},{96,64},{128,96},{160,128},{192,160},{224,192},{256... | collective-permute-start | bytes 49160 | tf_op jit(solution)/shard_map/ppermute | solution.py:23
  15.6 1.9 %collective-permute-start.4 = (bf16[1,2048]{1,0:T(2,128)(2,1)S(1)}, bf16[1,2048]{1,0:T(2,128)(2,1)S(1)}, u32[]{:S(2)}, u32[]{:S(2)}) collective-permute-start(bf16[1,2048]{1,0:T(2,128)(2,1)S(1)} %get-tuple-element.13), channel_id=1, source_target_pairs={{0,32},{32,64},{64,96},{96,128},{128,160},{160,192},{192,224},{224... | collective-permute-start | bytes 12296 | tf_op jit(solution)/shard_map/ppermute | solution.py:22
  17.5 5.5 %collective-permute-start.5 = (bf16[1,2048]{1,0:T(2,128)(2,1)S(1)}, bf16[1,2048]{1,0:T(2,128)(2,1)S(1)}, u32[]{:S(2)}, u32[]{:S(2)}) collective-permute-start(bf16[1,2048]{1,0:T(2,128)(2,1)S(1)} %get-tuple-element.14), channel_id=1, source_target_pairs={{32,0},{64,32},{96,64},{128,96},{160,128},{192,160},{224,192},{256... | collective-permute-start | bytes 12296 | tf_op jit(solution)/shard_map/ppermute | solution.py:23
  25.2 1.9 %collective-permute-start.2 = (f32[2,16,3,132]{3,2,1,0:T(4,128)S(1)}, f32[2,16,3,132]{3,2,1,0:T(4,128)S(1)}, u32[]{:S(2)}, u32[]{:S(2)}) collective-permute-start(f32[2,16,3,132]{3,2,1,0:T(4,128)S(1)} %get-tuple-element.5), channel_id=1, source_target_pairs={{0,1},{1,2},{2,3},{3,4},{4,5},{5,6},{6,7},{7,8},{8,9},{9,10},{10,1... | collective-permute-start | bytes 152072 | tf_op jit(solution)/shard_map/ppermute | solution.py:22
  27.2 1.3 collective-permute-start.3
  28.5 1.0 maximum_maximum_fusion.x0_ref
  29.5 3.5 %collective-permute-start.7 = (bf16[144,2048]{1,0:T(8,128)(2,1)}, bf16[144,2048]{1,0:T(8,128)(2,1)}, u32[]{:S(2)}, u32[]{:S(2)}) collective-permute-start(bf16[144,2048]{1,0:T(8,128)(2,1)} %maximum_maximum_fusion.x0_ref), channel_id=1, source_target_pairs={{0,256},{256,0},{1,257},{257,1},{2,258},{258,2},{3,259},{259,3},{4... | collective-permute-start | bytes 1769480 | tf_op jit(solution)/shard_map/ppermute | solution.py:96
  33.0 1.3 collective-permute-done.3
  34.2 1.0 pad_maximum_fusion
  35.5 4.3 %fusion.67 = (f32[16,68,130]{2,1,0:T(8,128)S(1)}, f32[16,68,130]{2,1,0:T(8,128)S(1)}) fusion(f32[16,70,132]{2,1,0:T(8,128)S(1)} %get-tuple-element.7, f32[16,70,132]{2,1,0:T(8,128)S(1)} %get-tuple-element.8), kind=kLoop, calls=%fused_computation.120 | loop fusion | flops 6223360 | bytes 15287296 | tf_op jit(solution)/shard_map/slice | solution.py:36
  39.8 2.1 %fusion.29 = bf16[16,66,128]{2,1,0:T(8,128)(2,1)S(1)} fusion(f32[16,68,130]{2,1,0:T(8,128)S(1)} %get-tuple-element.10, f32[16,70,132]{2,1,0:T(8,128)S(1)} %get-tuple-element.7, f32[16,68,130]{2,1,0:T(8,128)S(1)} %get-tuple-element.9), kind=kLoop, calls=%fused_computation.56 | loop fusion | flops 6082560 | bytes 8527872 | tf_op jit(solution)/shard_map/convert_element_type | solution.py:103
  42.2 1.2 broadcast_in_dim.15
  43.3 7.4 %all-to-all-start = ((bf16[16,272,128]{2,1,0:T(8,128)(2,1)}), bf16[16,272,128]{2,1,0:T(8,128)(2,1)S(1)}, u32[]{:S(2)}, u32[]{:S(2)}) async-start(bf16[16,272,128]{2,1,0:T(8,128)(2,1)} %bitcast.36), calls=%async_computation | async-start | bytes 2228224 | tf_op jit(solution)/shard_map/all_to_all | solution.py:113
  50.7 2.0 %collective-permute-start.6 = (bf16[144,2048]{1,0:T(8,128)(2,1)}, bf16[144,2048]{1,0:T(8,128)(2,1)S(1)}, u32[]{:S(2)}, u32[]{:S(2)}) collective-permute-start(bf16[144,2048]{1,0:T(8,128)(2,1)} %maximum_maximum_fusion.x0_ref), channel_id=1, source_target_pairs={{0,32},{32,0},{1,33},{33,1},{2,34},{34,2},{3,35},{35,3},{4,36},{36... | collective-permute-start | bytes 1769480 | tf_op jit(solution)/shard_map/ppermute | solution.py:97
  52.8 2.3 %collective-permute-start.8 = (bf16[144,2048]{1,0:T(8,128)(2,1)}, bf16[144,2048]{1,0:T(8,128)(2,1)}, u32[]{:S(2)}, u32[]{:S(2)}) collective-permute-start(bf16[144,2048]{1,0:T(8,128)(2,1)} %collective-permute-done.7.x2_ref), channel_id=1, source_target_pairs={{0,32},{32,0},{1,33},{33,1},{2,34},{34,2},{3,35},{35,3},{4,36},{36... | collective-permute-start | bytes 1769480 | tf_op jit(solution)/shard_map/ppermute | solution.py:97
  55.1 9.9 %all-to-all-done.got_ref = bf16[16,272,128]{2,1,0:T(8,128)(2,1)S(1)} async-done(((bf16[16,272,128]{2,1,0:T(8,128)(2,1)}), bf16[16,272,128]{2,1,0:T(8,128)(2,1)S(1)}, u32[]{:S(2)}, u32[]{:S(2)}) %all-to-all-start) | async-done | bytes 1114144 | tf_op jit(solution)/shard_map/all_to_all | solution.py:113
  65.0 1.0 copy-done.3
  66.0 5.1 %solve_x.1 = f32[4,272,128]{2,1,0:T(8,128)} custom-call(s32[1]{0:T(128)} %bitcast.block_ref, bf16[16,272,128]{2,1,0:T(8,128)(2,1)} %copy-done.3, bf16[144,2048]{1,0:T(8,128)(2,1)} %maximum_maximum_fusion.x0_ref, bf16[144,2048]{1,0:T(8,128)(2,1)} %copy-done.7, bf16[144,2048]{1,0:T(8,128)(2,1)} %collective-permute-done.7.x2_ref, ...), custom_call_target="tpu_custom_call" | custom-call | tf_op jit(solution)/shard_map/solve_x/pallas_call | solution.py:72
  71.1 3.5 %all-to-all-start.1 = ((f32[4,272,128]{2,1,0:T(8,128)}), f32[4,272,128]{2,1,0:T(8,128)S(1)}, u32[]{:S(2)}, u32[]{:S(2)}) async-start(f32[4,272,128]{2,1,0:T(8,128)} %solve_x.1), calls=%async_computation.1 | async-start | bytes 1114112 | tf_op jit(solution)/shard_map/all_to_all | solution.py:116
  75.0 8.8 %all-to-all-done.1 = f32[4,272,128]{2,1,0:T(8,128)S(1)} async-done(((f32[4,272,128]{2,1,0:T(8,128)}), f32[4,272,128]{2,1,0:T(8,128)S(1)}, u32[]{:S(2)}, u32[]{:S(2)}) %all-to-all-start.1) | async-done | bytes 557088 | tf_op jit(solution)/shard_map/all_to_all | solution.py:116
  83.9 17.0 %all-gather.2.cloned.1.call-done = bf16[1024,1024]{1,0:T(8,128)(2,1)} async-done(((bf16[64,1024]{1,0:T(8,128)(2,1)}), bf16[1024,1024]{1,0:T(8,128)(2,1)}) %all-gather.2.cloned.1.call-update) | async-done | bytes 2097168 | tf_op jit(solution)/shard_map/all_gather | solution.py:88
  100.8 2.1 %collective-permute-start.10 = (bf16[1024,1024]{1,0:T(8,128)(2,1)}, bf16[1024,1024]{1,0:T(8,128)(2,1)}, u32[]{:S(2)}, u32[]{:S(2)}) collective-permute-start(bf16[1024,1024]{1,0:T(8,128)(2,1)} %all-gather.2.cloned.1.call-done), channel_id=1, source_target_pairs={{0,32},{32,0},{1,33},{33,1},{2,34},{34,2},{3,35},{35,3},{4,36},{36... | collective-permute-start | bytes 6291464 | tf_op jit(solution)/shard_map/ppermute | solution.py:89
  103.3 1.1 copy.36
  104.4 1.1 slice.284
  106.3 1.9 %fusion.49 = bf16[16,64,128]{2,1,0:T(8,128)(2,1)S(1)} fusion(f32[16,64,128]{2,1,0:T(8,128)S(1)} %bitcast.29, f32[16,66,130]{2,1,0:T(8,128)S(1)} %multiply_subtract_fusion, f32[16,70,132]{2,1,0:T(8,128)S(1)} %get-tuple-element.7, f32[16,66,130]{2,1,0:T(8,128)S(1)} %slice.286), kind=kLoop, calls=%fused_computation.85 | loop fusion | flops 5898240 | bytes 8388608 | tf_op jit(solution)/shard_map/convert_element_type | solution.py:126
  108.2 26.4 %all_to_all.20 = bf16[16,64,128]{2,1,0:T(8,128)(2,1)S(1)} all-to-all(bf16[16,64,128]{2,1,0:T(8,128)(2,1)S(1)} %fusion.49), channel_id=1, replica_groups=mesh['yl'=2,'x'=4,'c'=2,'yh'=2,'z'=16] {'z'}, dimensions={0} | all-to-all | bytes 524288 | tf_op jit(solution)/shard_map/all_to_all | solution.py:128
  134.6 4.7 %collective-permute-start.9 = (bf16[1024,128]{1,0:T(8,128)(2,1)S(1)}, bf16[1024,128]{1,0:T(8,128)(2,1)S(1)}, u32[]{:S(2)}, u32[]{:S(2)}) collective-permute-start(bf16[1024,128]{1,0:T(8,128)(2,1)S(1)} %bitcast.37), channel_id=1, source_target_pairs={{0,16},{16,0},{1,17},{17,1},{2,18},{18,2},{3,19},{19,3},{4,20},{20... | collective-permute-start | bytes 786440 | tf_op jit(solution)/shard_map/ppermute | solution.py:129
  139.3 5.0 %collective-permute-done.9 = bf16[1024,128]{1,0:T(8,128)(2,1)S(1)} collective-permute-done((bf16[1024,128]{1,0:T(8,128)(2,1)S(1)}, bf16[1024,128]{1,0:T(8,128)(2,1)S(1)}, u32[]{:S(2)}, u32[]{:S(2)}) %collective-permute-start.9) | collective-permute-done | bytes 262176 | tf_op jit(solution)/shard_map/ppermute | solution.py:129
  144.3 2.3 %fusion.60 = f32[1024,128]{1,0:T(8,128)S(1)} fusion(bf16[1024,1024]{1,0:T(8,128)(2,1)} %collective-permute-done.10, bf16[1024,128]{1,0:T(8,128)(2,1)S(1)} %collective-permute-done.9, bf16[1024,128]{1,0:T(8,128)(2,1)S(1)} %bitcast.38, pred[]{:T(512)S(6)} %eq.3), kind=kOutput, calls=%fused_computation.105 | convolution fusion | flops 268566528 | bytes 3145729 | tf_op jit(solution)/shard_map/dot_general | solution.py:133
  147.4 25.7 %all_to_all.21 = bf16[16,64,128]{2,1,0:T(8,128)(2,1)S(1)} all-to-all(bf16[16,64,128]{2,1,0:T(8,128)(2,1)S(1)} %bitcast.40), channel_id=1, replica_groups=mesh['yl'=2,'x'=4,'c'=2,'yh'=2,'z'=16] {'z'}, dimensions={0} | all-to-all | bytes 524288 | tf_op jit(solution)/shard_map/all_to_all | solution.py:135
  (56 shorter events, 7.2 us)
Async XLA Ops:
  6.5 16.5 %copy-start = (bf16[64,2048]{1,0:T(8,128)(2,1)S(1)}, bf16[64,2048]{1,0:T(8,128)(2,1)}, u32[]{:S(2)}) copy-start(bf16[64,2048]{1,0:T(8,128)(2,1)} %param.7) | copy-start | bytes 786436
  6.5 94.3 %all-gather.2.cloned.1.call-start = ((), (), s32[]{:S(2)}) async-start(), calls=%async_computation.4 | async-start | bytes 2228224 | tf_op jit(solution)/shard_map/all_gather | solution.py:88
  8.8 15.1 %collective-permute-start = (f32[2,16,64,2]{2,1,3,0:T(8,128)S(1)}, f32[2,16,64,2]{2,1,3,0:T(8,128)S(1)}, u32[]{:S(2)}, u32[]{:S(2)}) collective-permute-start(f32[2,16,64,2]{2,1,3,0:T(8,128)S(1)} %copy.29), channel_id=1, source_target_pairs={{0,32},{32,64},{64,96},{96,128},{128,160},{160,192},{192,224},{224... | collective-permute-start | bytes 49160 | tf_op jit(solution)/shard_map/ppermute | solution.py:22
  11.1 13.2 %collective-permute-start.1 = (f32[2,16,64,2]{2,1,3,0:T(8,128)S(1)}, f32[2,16,64,2]{2,1,3,0:T(8,128)S(1)}, u32[]{:S(2)}, u32[]{:S(2)}) collective-permute-start(f32[2,16,64,2]{2,1,3,0:T(8,128)S(1)} %copy.30), channel_id=1, source_target_pairs={{32,0},{64,32},{96,64},{128,96},{160,128},{192,160},{224,192},{256... | collective-permute-start | bytes 49160 | tf_op jit(solution)/shard_map/ppermute | solution.py:23
  15.6 12.9 %collective-permute-start.4 = (bf16[1,2048]{1,0:T(2,128)(2,1)S(1)}, bf16[1,2048]{1,0:T(2,128)(2,1)S(1)}, u32[]{:S(2)}, u32[]{:S(2)}) collective-permute-start(bf16[1,2048]{1,0:T(2,128)(2,1)S(1)} %get-tuple-element.13), channel_id=1, source_target_pairs={{0,32},{32,64},{64,96},{96,128},{128,160},{160,192},{192,224},{224... | collective-permute-start | bytes 12296 | tf_op jit(solution)/shard_map/ppermute | solution.py:22
  17.5 11.0 %collective-permute-start.5 = (bf16[1,2048]{1,0:T(2,128)(2,1)S(1)}, bf16[1,2048]{1,0:T(2,128)(2,1)S(1)}, u32[]{:S(2)}, u32[]{:S(2)}) collective-permute-start(bf16[1,2048]{1,0:T(2,128)(2,1)S(1)} %get-tuple-element.14), channel_id=1, source_target_pairs={{32,0},{64,32},{96,64},{128,96},{160,128},{192,160},{224,192},{256... | collective-permute-start | bytes 12296 | tf_op jit(solution)/shard_map/ppermute | solution.py:23
  23.8 1.0 copy-start.1
  23.8 1.2 copy-start.2
  25.0 3.5 %copy-start.8 = (bf16[128,2048]{1,0:T(8,128)(2,1)S(1)}, bf16[128,2048]{1,0:T(8,128)(2,1)}, u32[]{:S(2)}) copy-start(bf16[128,2048]{1,0:T(8,128)(2,1)} %param.6) | copy-start | bytes 1572868
  25.2 7.7 %collective-permute-start.2 = (f32[2,16,3,132]{3,2,1,0:T(4,128)S(1)}, f32[2,16,3,132]{3,2,1,0:T(4,128)S(1)}, u32[]{:S(2)}, u32[]{:S(2)}) collective-permute-start(f32[2,16,3,132]{3,2,1,0:T(4,128)S(1)} %get-tuple-element.5), channel_id=1, source_target_pairs={{0,1},{1,2},{2,3},{3,4},{4,5},{5,6},{6,7},{7,8},{8,9},{9,10},{10,1... | collective-permute-start | bytes 152072 | tf_op jit(solution)/shard_map/ppermute | solution.py:22
  27.2 7.1 %collective-permute-start.3 = (f32[2,16,3,132]{3,2,1,0:T(4,128)S(1)}, f32[2,16,3,132]{3,2,1,0:T(4,128)S(1)}, u32[]{:S(2)}, u32[]{:S(2)}) collective-permute-start(f32[2,16,3,132]{3,2,1,0:T(4,128)S(1)} %get-tuple-element.6), channel_id=1, source_target_pairs={{1,0},{2,1},{3,2},{4,3},{5,4},{6,5},{7,6},{8,7},{9,8},{10,9},{11,1... | collective-permute-start | bytes 152072 | tf_op jit(solution)/shard_map/ppermute | solution.py:23
  29.5 23.3 %collective-permute-start.7 = (bf16[144,2048]{1,0:T(8,128)(2,1)}, bf16[144,2048]{1,0:T(8,128)(2,1)}, u32[]{:S(2)}, u32[]{:S(2)}) collective-permute-start(bf16[144,2048]{1,0:T(8,128)(2,1)} %maximum_maximum_fusion.x0_ref), channel_id=1, source_target_pairs={{0,256},{256,0},{1,257},{257,1},{2,258},{258,2},{3,259},{259,3},{4... | collective-permute-start | bytes 1769480 | tf_op jit(solution)/shard_map/ppermute | solution.py:96
  43.3 21.6 %all-to-all-start = ((bf16[16,272,128]{2,1,0:T(8,128)(2,1)}), bf16[16,272,128]{2,1,0:T(8,128)(2,1)S(1)}, u32[]{:S(2)}, u32[]{:S(2)}) async-start(bf16[16,272,128]{2,1,0:T(8,128)(2,1)} %bitcast.36), calls=%async_computation | async-start | bytes 2228224 | tf_op jit(solution)/shard_map/all_to_all | solution.py:113
  50.7 4.4 %collective-permute-start.6 = (bf16[144,2048]{1,0:T(8,128)(2,1)}, bf16[144,2048]{1,0:T(8,128)(2,1)S(1)}, u32[]{:S(2)}, u32[]{:S(2)}) collective-permute-start(bf16[144,2048]{1,0:T(8,128)(2,1)} %maximum_maximum_fusion.x0_ref), channel_id=1, source_target_pairs={{0,32},{32,0},{1,33},{33,1},{2,34},{34,2},{3,35},{35,3},{4,36},{36... | collective-permute-start | bytes 1769480 | tf_op jit(solution)/shard_map/ppermute | solution.py:97
  52.8 12.2 %collective-permute-start.8 = (bf16[144,2048]{1,0:T(8,128)(2,1)}, bf16[144,2048]{1,0:T(8,128)(2,1)}, u32[]{:S(2)}, u32[]{:S(2)}) collective-permute-start(bf16[144,2048]{1,0:T(8,128)(2,1)} %collective-permute-done.7.x2_ref), channel_id=1, source_target_pairs={{0,32},{32,0},{1,33},{33,1},{2,34},{34,2},{3,35},{35,3},{4,36},{36... | collective-permute-start | bytes 1769480 | tf_op jit(solution)/shard_map/ppermute | solution.py:97
  55.1 9.9 %copy-start.7 = (bf16[144,2048]{1,0:T(8,128)(2,1)}, bf16[144,2048]{1,0:T(8,128)(2,1)S(1)}, u32[]{:S(2)}) copy-start(bf16[144,2048]{1,0:T(8,128)(2,1)S(1)} %collective-permute-done.6.x1_ref) | copy-start | bytes 1769476
  65.0 1.0 copy-start.3
  71.1 12.6 %all-to-all-start.1 = ((f32[4,272,128]{2,1,0:T(8,128)}), f32[4,272,128]{2,1,0:T(8,128)S(1)}, u32[]{:S(2)}, u32[]{:S(2)}) async-start(f32[4,272,128]{2,1,0:T(8,128)} %solve_x.1), calls=%async_computation.1 | async-start | bytes 1114112 | tf_op jit(solution)/shard_map/all_to_all | solution.py:116
  83.7 19.3 %copy-start.5 = (f32[4,272,128]{2,1,0:T(8,128)}, f32[4,272,128]{2,1,0:T(8,128)S(1)}, u32[]{:S(2)}) copy-start(f32[4,272,128]{2,1,0:T(8,128)S(1)} %all-to-all-done.1) | copy-start | bytes 1671172
  100.8 43.5 %collective-permute-start.10 = (bf16[1024,1024]{1,0:T(8,128)(2,1)}, bf16[1024,1024]{1,0:T(8,128)(2,1)}, u32[]{:S(2)}, u32[]{:S(2)}) collective-permute-start(bf16[1024,1024]{1,0:T(8,128)(2,1)} %all-gather.2.cloned.1.call-done), channel_id=1, source_target_pairs={{0,32},{32,0},{1,33},{33,1},{2,34},{34,2},{3,35},{35,3},{4,36},{36... | collective-permute-start | bytes 6291464 | tf_op jit(solution)/shard_map/ppermute | solution.py:89
  104.4 1.2 copy-start.4
  134.6 9.8 %collective-permute-start.9 = (bf16[1024,128]{1,0:T(8,128)(2,1)S(1)}, bf16[1024,128]{1,0:T(8,128)(2,1)S(1)}, u32[]{:S(2)}, u32[]{:S(2)}) collective-permute-start(bf16[1024,128]{1,0:T(8,128)(2,1)S(1)} %bitcast.37), channel_id=1, source_target_pairs={{0,16},{16,0},{1,17},{17,1},{2,18},{18,2},{3,19},{19,3},{4,20},{20... | collective-permute-start | bytes 786440 | tf_op jit(solution)/shard_map/ppermute | solution.py:129
  139.3 7.3 %copy-start.6 = (bf16[1024,1024]{1,0:T(8,128)(2,1)S(1)}, bf16[1024,1024]{1,0:T(8,128)(2,1)}, u32[]{:S(2)}) copy-start(bf16[1024,1024]{1,0:T(8,128)(2,1)} %all-gather.2.cloned.1.call-done) | copy-start | bytes 6291460
Sparse Core Ops, SparseCore 0:
  23.9 76.8 all-gather.1
